TPU v7x, 32 devices: a whole 2x2x4 slice. The times are simulated.
32 devices in a mesh: groups: 2 (over y), ctx: 4 (over z), dom: 2 (over x), tp: 2 (over core).
Axes of the slice: x: 2, y: 2, z: 4, core: 2. Of those that a mesh axis runs over, the one named last changes fastest.
Arguments:
- queries: bfloat16 [8, 32, 8, 8, 128], P('groups', 'dom', 'tp'), parts along dimension 0, may hold values from -8 to 8
- prompt_cache: bfloat16 [4, 8192, 8, 128], P('groups', 'ctx', 'tp'), parts along dimension 0, may hold values from -8 to 8
- suffix_cache: bfloat16 [4, 32, 16, 8, 128], P('groups', 'dom', 'ctx', 'tp'), parts along dimension 0, may hold values from -8 to 8
- new_kv: bfloat16 [8, 2, 32, 8, 128], P('groups', None, 'dom', 'tp'), parts along dimension 0, may hold values from -8 to 8
- ancestors: int32 [8, 32], P('groups'), parts along dimension 0, may hold values from 0 to 31, as said below
- lengths: int32 [64], P('groups'), parts along dimension 0, may hold values from 1 to 12, as said below
Outputs:
- attended: bfloat16 [8, 32, 8, 8, 128], P('groups', 'dom', 'tp'), parts along dimension 0
There are 2 independent parts, one for each index of `groups`. A program takes and returns all parts, laid end to end along the dimension named above; each array names one. Nothing has to cross between parts.
Inputs may be any that keep to these rules, and one draw needn't show every extreme that they name: `ancestors`: particle p is owned by owner p // 16. In every step, of the 16 offspring of one owner at most 16 have their ancestor among the particles of any one owner, and each owner has exactly 16 from some one owner. `lengths`: the largest length is reached in every draw.
All inputs are finite; a program needn't handle non-finite values.
Results may differ from a plain program's by a relative error of at most 0.005.
Values may be sent and summed in bfloat16 or wider, within the bound.
A program may use at most 128 MiB of HBM per device.

v0:
```python
import math

import jax
import jax.numpy as jnp
from jax import lax
from jax.sharding import PartitionSpec as P


def resample_whole(flat_rows, my_parents, particles):
    one_hot = (my_parents[:, None] == jnp.arange(particles, dtype=jnp.int32)[None, :]).astype(
        jnp.bfloat16
    )
    gathered = jnp.einsum(
        "ji,cir->cjr",
        one_hot,
        lax.all_gather(flat_rows, "dom", axis=1, tiled=True),
        preferred_element_type=jnp.float32,
    )
    return gathered.astype(jnp.bfloat16)


def attend(query_block, prompt_keys, prompt_values, suffix_rows, visible, score_scale):
    prompt_scores = (
        jnp.einsum("pkgh,tkh->kpgt", query_block, prompt_keys, preferred_element_type=jnp.float32)
        * score_scale
    )
    suffix_scores = (
        jnp.einsum(
            "pkgh,pskh->pkgs", query_block, suffix_rows[0], preferred_element_type=jnp.float32
        )
        * score_scale
    )
    suffix_scores = jnp.where(visible[:, None, None, :], suffix_scores, -jnp.inf)
    local_peak = jnp.maximum(
        jnp.transpose(jnp.max(prompt_scores, axis=-1), (1, 0, 2)), jnp.max(suffix_scores, axis=-1)
    )
    peak_score = lax.pmax(local_peak, "ctx")
    prompt_exp = jnp.exp(prompt_scores - jnp.transpose(peak_score, (1, 0, 2))[..., None])
    suffix_exp = jnp.exp(suffix_scores - peak_score[..., None])
    totals = jnp.transpose(jnp.sum(prompt_exp, axis=-1), (1, 0, 2)) + jnp.sum(suffix_exp, axis=-1)
    prompt_weights = prompt_exp.astype(jnp.bfloat16)
    suffix_weights = suffix_exp.astype(jnp.bfloat16)
    numerator = jnp.einsum(
        "kpgt,tkh->pkgh", prompt_weights, prompt_values, preferred_element_type=jnp.float32
    )
    numerator = numerator + jnp.einsum(
        "pkgs,pskh->pkgh", suffix_weights, suffix_rows[1], preferred_element_type=jnp.float32
    )
    total_all, numerator_all = lax.psum((totals, numerator), "ctx")
    return (numerator_all / total_all[..., None]).astype(jnp.bfloat16)


def on_device(queries, prompt_cache, suffix_cache, new_kv, ancestors, lengths):
    my_owner = lax.axis_index("dom")
    my_shard = lax.axis_index("ctx")
    per_owner = queries.shape[1]
    suffix_dev = suffix_cache.shape[2]
    particles = ancestors.shape[1]
    score_scale = 1.0 / math.sqrt(queries.shape[4])
    prompt_keys = prompt_cache[0]
    prompt_values = prompt_cache[1]
    particle_ids = jnp.arange(particles, dtype=jnp.int32)
    positions = my_shard * suffix_dev + jnp.arange(suffix_dev, dtype=jnp.int32)
    suffix_rows = suffix_cache
    lengths_now = lengths
    results = []
    for step_index in range(queries.shape[0]):
        parents = ancestors[step_index]
        my_parents = lax.dynamic_slice_in_dim(parents, my_owner * per_owner, per_owner)
        flat_rows = suffix_rows.reshape(2, per_owner, -1)
        moved_rows = resample_whole(flat_rows, my_parents, particles)
        suffix_rows = moved_rows.reshape(suffix_rows.shape)
        lengths_now = jnp.sum(
            jnp.where(parents[:, None] == particle_ids[None, :], lengths_now[None, :], 0), axis=1
        )
        my_lengths = lax.dynamic_slice_in_dim(lengths_now, my_owner * per_owner, per_owner)
        new_slot = positions[None, :] == my_lengths[:, None]
        suffix_rows = jnp.where(
            new_slot[None, :, :, None, None], new_kv[step_index][:, :, None], suffix_rows
        )
        visible = positions[None, :] <= my_lengths[:, None]
        results.append(
            attend(
                queries[step_index], prompt_keys, prompt_values, suffix_rows, visible, score_scale
            )
        )
        lengths_now = lengths_now + 1
    return jnp.stack(results)


def solution(mesh):
    return jax.shard_map(
        on_device,
        mesh=mesh,
        in_specs=(
            P("groups", "dom", "tp", None, None),
            P("groups", "ctx", "tp", None),
            P("groups", "dom", "ctx", "tp", None),
            P("groups", None, "dom", "tp", None),
            P("groups", None),
            P("groups"),
        ),
        out_specs=P("groups", "dom", "tp", None, None),
        check_vma=False,
    )
```

profile of v0, /device:TPU:0, one launch (start us, length us, event | category | flops | bytes accessed | tf_op | source)
XLA Modules:
  0.0 163.5 jit_solution(15562038349087660170)
XLA Ops:
  8.8 4.1 %fusion.100 = (bf16[1,2048,4,128]{3,2,1,0:T(4,128)(2,1)S(1)}, bf16[1,2048,4,128]{3,2,1,0:T(4,128)(2,1)}) fusion(bf16[2,2048,4,128]{3,2,1,0:T(4,128)(2,1)} %param.7), kind=kLoop, calls=%fused_computation.178 | loop fusion | bytes 8388608 | tf_op jit(solution)/shard_map/slice | solution.py:60
  17.0 7.1 %all_gather.12 = bf16[2,32,2048]{2,1,0:T(8,128)(2,1)S(1)} all-gather(bf16[2,16,2048]{2,1,0:T(8,128)(2,1)S(1)} %reshape.274), channel_id=1, replica_groups=mesh['groups'=2,'ctx'=4,'dom'=2,'tp'=2] {'dom'}, dimensions={1}, use_global_device_ids=true | all-gather | bytes 393216 | tf_op jit(solution)/shard_map/all_gather | solution.py:16
  24.4 5.6 %all_gather.13 = bf16[2,32,2048]{2,1,0:T(8,128)(2,1)S(1)} all-gather(bf16[2,16,2048]{2,1,0:T(8,128)(2,1)S(1)} %get-tuple-element.59), channel_id=1, replica_groups=mesh['groups'=2,'ctx'=4,'dom'=2,'tp'=2] {'dom'}, dimensions={1}, use_global_device_ids=true | all-gather | bytes 393216 | tf_op jit(solution)/shard_map/all_gather | solution.py:16
  30.4 5.6 %all_gather.14 = bf16[2,32,2048]{2,1,0:T(8,128)(2,1)S(1)} all-gather(bf16[2,16,2048]{2,1,0:T(8,128)(2,1)S(1)} %get-tuple-element.61), channel_id=1, replica_groups=mesh['groups'=2,'ctx'=4,'dom'=2,'tp'=2] {'dom'}, dimensions={1}, use_global_device_ids=true | all-gather | bytes 393216 | tf_op jit(solution)/shard_map/all_gather | solution.py:16
  36.3 5.8 %all_gather.15 = bf16[2,32,2048]{2,1,0:T(8,128)(2,1)S(1)} all-gather(bf16[2,16,2048]{2,1,0:T(8,128)(2,1)S(1)} %get-tuple-element.63), channel_id=1, replica_groups=mesh['groups'=2,'ctx'=4,'dom'=2,'tp'=2] {'dom'}, dimensions={1}, use_global_device_ids=true | all-gather | bytes 393216 | tf_op jit(solution)/shard_map/all_gather | solution.py:16
  42.5 4.1 %multiply_reduce_fusion = (f32[4,16,8]{2,1,0:T(8,128)}, f32[4,16,8,2048]{3,2,1,0:T(8,128)}) fusion(bf16[1,2048,4,128]{3,2,1,0:T(4,128)(2,1)S(1)} %get-tuple-element.17, bf16[1,16,4,8,128]{4,3,2,1,0:T(8,128)(2,1)} %get-tuple-element.22), kind=kOutput, calls=%fused_computation.4 | convolution fusion | flops 270532096 | bytes 6424576 | tf_op jit(solution)/shard_map/pkgh,tkh->kpgt/dot_general | solution.py:24
  46.7 3.3 %multiply_reduce_fusion.1 = (f32[4,16,8]{2,1,0:T(8,128)}, f32[4,16,8,2048]{3,2,1,0:T(8,128)}) fusion(bf16[1,2048,4,128]{3,2,1,0:T(4,128)(2,1)S(1)} %get-tuple-element.17, bf16[1,16,4,8,128]{4,3,2,1,0:T(8,128)(2,1)S(1)} %copy-done.10), kind=kOutput, calls=%fused_computation.5 | convolution fusion | flops 270532096 | bytes 6424576 | tf_op jit(solution)/shard_map/pkgh,tkh->kpgt/dot_general | solution.py:24
  50.0 3.3 %multiply_reduce_fusion.2 = (f32[4,16,8]{2,1,0:T(8,128)}, f32[4,16,8,2048]{3,2,1,0:T(8,128)}) fusion(bf16[1,2048,4,128]{3,2,1,0:T(4,128)(2,1)S(1)} %get-tuple-element.17, bf16[1,16,4,8,128]{4,3,2,1,0:T(8,128)(2,1)S(1)} %copy-done.9), kind=kOutput, calls=%fused_computation.6 | convolution fusion | flops 270532096 | bytes 6424576 | tf_op jit(solution)/shard_map/pkgh,tkh->kpgt/dot_general | solution.py:24
  53.5 2.7 %multiply_reduce_fusion.3 = (f32[4,16,8]{2,1,0:T(8,128)S(1)}, f32[4,16,8,2048]{3,2,1,0:T(8,128)}) fusion(bf16[1,2048,4,128]{3,2,1,0:T(4,128)(2,1)S(1)} %get-tuple-element.17, bf16[1,16,4,8,128]{4,3,2,1,0:T(8,128)(2,1)S(1)} %copy-done.8), kind=kOutput, calls=%fused_computation.7 | convolution fusion | flops 270532096 | bytes 6424576 | tf_op jit(solution)/shard_map/pkgh,tkh->kpgt/dot_general | solution.py:24
  56.2 1.1 copy_select_fusion
  57.3 1.6 fusion.102
  58.9 1.4 bitcast_maximum_fusion
  63.2 22.2 %all-reduce.2 = (f32[16,4,8]{2,0,1:T(8,128)S(1)}, f32[16,4,8]{2,0,1:T(8,128)S(1)}, f32[16,4,8]{2,0,1:T(8,128)S(1)}, f32[16,4,8]{2,0,1:T(8,128)S(1)}) all-reduce(f32[16,4,8]{2,0,1:T(8,128)} %bitcast_maximum_fusion, f32[16,4,8]{2,0,1:T(8,128)} %bitcast_maximum_fusion.1, ...), channel_id=1, replica_groups=mesh['groups'=2,'ctx'=4,'dom'=2,'tp'=2] {'ctx'}, use_global_device_ids=true, to_apply=%region_27.28 | all-reduce | flops 2048 | bytes 16384 | tf_op jit(solution)/shard_map/pmax | solution.py:37
  86.6 3.4 %fusion.41 = f32[16,4,8,128]{3,2,0,1:T(8,128)S(1)} fusion(bf16[1,2048,4,128]{3,2,1,0:T(4,128)(2,1)S(1)} %copy-done.6, f32[4,16,8,2048]{3,2,1,0:T(8,128)} %get-tuple-element.58, f32[4,16,8]{2,1,0:T(8,128)S(1)} %bitcast.214), kind=kOutput, calls=%fused_computation.49 | convolution fusion | flops 271581184 | bytes 6555648 | tf_op jit(solution)/shard_map/kpgt,tkh->pkgh/dot_general | solution.py:43
  91.0 1.1 fusion.38
  93.2 1.1 fusion.35
  95.4 1.1 fusion.32
  97.7 3.2 %fusion.6 = f32[4,16,8]{2,1,0:T(8,128)S(1)} fusion(f32[4,16,8,2048]{3,2,1,0:T(8,128)} %get-tuple-element.58, f32[4,16,8]{2,1,0:T(8,128)S(1)} %bitcast.215), kind=kLoop, calls=%fused_computation.14 | loop fusion | flops 3145216 | bytes 4198400 | tf_op jit(solution)/shard_map/reduce_sum | solution.py:40
  104.8 21.4 %all-reduce = (f32[16,4,8]{2,0,1:T(8,128)S(1)}, f32[16,4,8]{2,0,1:T(8,128)S(1)}, f32[16,4,8]{2,0,1:T(8,128)S(1)}, f32[16,4,8]{2,0,1:T(8,128)S(1)}) all-reduce(f32[16,4,8]{2,0,1:T(8,128)S(1)} %bitcast_add_fusion, f32[16,4,8]{2,0,1:T(8,128)S(1)} %bitcast_add_fusion.1, ...), channel_id=1, replica_groups=mesh['groups'=2,'ctx'=4,'dom'=2,'tp'=2] {'ctx'}, use_global_device_ids=true, to_apply=%region_31.32 | all-reduce | flops 2048 | bytes 16384 | tf_op jit(solution)/shard_map/psum | solution.py:49
  126.2 25.2 %all-reduce.5.cloned.1.call-done = (f32[16,4,8,128]{3,2,0,1:T(8,128)}, f32[16,4,8,128]{3,2,0,1:T(8,128)}, f32[16,4,8,128]{3,2,0,1:T(8,128)}, f32[16,4,8,128]{3,2,0,1:T(8,128)}) async-done(((f32[16,4,8,128]{3,2,0,1:T(8,128)}, f32[16,4,8,128]{3,2,0,1:T(8,128)}, f32[16,4,8,128]{3,2,0,1:T(8,128)}, f32[16,4,8,128]{3,2,0,1:T(8,128)}), (f32[16,4,8,128]{3,2,0,1:T(8,128)}, f32[16,4,8,128]{3,2,0,1:T(8,128)}, ...) | async-done | bytes 1048592 | tf_op jit(solution)/shard_map/psum | solution.py:49
  151.3 1.1 fusion.59
  152.4 1.1 fusion.58
  153.5 1.1 fusion.57
  154.6 1.1 fusion.56
  (115 shorter events, 21.1 us)
Async XLA Ops:
  6.5 144.8 %all-reduce.5.cloned.1.call-start = ((), (), s32[]{:S(2)}) async-start(), calls=%async_computation | async-start | bytes 2097152 | tf_op jit(solution)/shard_map/psum | solution.py:49
  8.8 4.1 %copy-start.7 = (bf16[4,16,4,8,128]{4,3,2,1,0:T(8,128)(2,1)S(1)}, bf16[4,16,4,8,128]{4,3,2,1,0:T(8,128)(2,1)}, u32[]{:S(2)}) copy-start(bf16[4,16,4,8,128]{4,3,2,1,0:T(8,128)(2,1)} %param.6) | copy-start | bytes 1572868
  8.8 4.9 %copy-start.18 = (bf16[4,2,16,4,128]{4,3,2,1,0:T(4,128)(2,1)S(1)}, bf16[4,2,16,4,128]{4,3,2,1,0:T(4,128)(2,1)}, u32[]{:S(2)}) copy-start(bf16[4,2,16,4,128]{4,3,2,1,0:T(4,128)(2,1)} %param.9) | copy-start | bytes 393220
  8.8 8.1 %copy-start.19 = (bf16[2,16,4,4,128]{4,3,2,1,0:T(4,128)(2,1)S(1)}, bf16[2,16,4,4,128]{4,3,2,1,0:T(4,128)(2,1)}, u32[]{:S(2)}) copy-start(bf16[2,16,4,4,128]{4,3,2,1,0:T(4,128)(2,1)} %param.8) | copy-start | bytes 393220
  14.4 0.6 copy-start.15
  14.4 2.2 %copy-start.11 = (bf16[2,16,4,128]{3,2,1,0:T(4,128)(2,1)}, bf16[2,16,4,128]{3,2,1,0:T(4,128)(2,1)S(1)}, u32[]{:S(2)}) copy-start(bf16[2,16,4,128]{3,2,1,0:T(4,128)(2,1)S(1)} %get-tuple-element.32) | copy-start | bytes 98308
  14.4 2.2 %copy-start.13 = (bf16[2,16,4,128]{3,2,1,0:T(4,128)(2,1)}, bf16[2,16,4,128]{3,2,1,0:T(4,128)(2,1)S(1)}, u32[]{:S(2)}) copy-start(bf16[2,16,4,128]{3,2,1,0:T(4,128)(2,1)S(1)} %get-tuple-element.33) | copy-start | bytes 98308
  36.3 10.4 %copy-start.10 = (bf16[1,16,4,8,128]{4,3,2,1,0:T(8,128)(2,1)S(1)}, bf16[1,16,4,8,128]{4,3,2,1,0:T(8,128)(2,1)}, u32[]{:S(2)}) copy-start(bf16[1,16,4,8,128]{4,3,2,1,0:T(8,128)(2,1)} %get-tuple-element.20) | copy-start | bytes 393220
  46.7 3.3 %copy-start.9 = (bf16[1,16,4,8,128]{4,3,2,1,0:T(8,128)(2,1)S(1)}, bf16[1,16,4,8,128]{4,3,2,1,0:T(8,128)(2,1)}, u32[]{:S(2)}) copy-start(bf16[1,16,4,8,128]{4,3,2,1,0:T(8,128)(2,1)} %get-tuple-element.21) | copy-start | bytes 393220
  50.0 3.5 %copy-start.8 = (bf16[1,16,4,8,128]{4,3,2,1,0:T(8,128)(2,1)S(1)}, bf16[1,16,4,8,128]{4,3,2,1,0:T(8,128)(2,1)}, u32[]{:S(2)}) copy-start(bf16[1,16,4,8,128]{4,3,2,1,0:T(8,128)(2,1)} %get-tuple-element.19) | copy-start | bytes 393220
  53.4 7.8 %copy-start.17 = (f32[4,16,8]{2,1,0:T(8,128)S(1)}, f32[4,16,8]{2,1,0:T(8,128)}, u32[]{:S(2)}) copy-start(f32[4,16,8]{2,1,0:T(8,128)} %get-tuple-element.67) | copy-start | bytes 6148
  53.5 8.4 %copy-start.12 = (bf16[2,16,4,128]{3,2,1,0:T(4,128)(2,1)S(1)}, bf16[2,16,4,128]{3,2,1,0:T(4,128)(2,1)}, u32[]{:S(2)}) copy-start(bf16[2,16,4,128]{3,2,1,0:T(4,128)(2,1)} %copy-done.11) | copy-start | bytes 98308
  53.5 8.4 %copy-start.14 = (bf16[2,16,4,128]{3,2,1,0:T(4,128)(2,1)S(1)}, bf16[2,16,4,128]{3,2,1,0:T(4,128)(2,1)}, u32[]{:S(2)}) copy-start(bf16[2,16,4,128]{3,2,1,0:T(4,128)(2,1)} %copy-done.13) | copy-start | bytes 98308
  53.5 8.6 %copy-start.21 = (pred[16,4]{1,0:T(8,128)(4,1)S(1)}, pred[16,4]{1,0:T(8,128)(4,1)}, u32[]{:S(2)}) copy-start(pred[16,4]{1,0:T(8,128)(4,1)} %get-tuple-element.52) | copy-start | bytes 196
  53.5 8.8 %copy-start.16 = (f32[4,16,8]{2,1,0:T(8,128)S(1)}, f32[4,16,8]{2,1,0:T(8,128)}, u32[]{:S(2)}) copy-start(f32[4,16,8]{2,1,0:T(8,128)} %get-tuple-element.71) | copy-start | bytes 6148
  53.5 9.5 %copy-start.20 = (pred[16,4]{1,0:T(8,128)(4,1)S(1)}, pred[16,4]{1,0:T(8,128)(4,1)}, u32[]{:S(2)}) copy-start(pred[16,4]{1,0:T(8,128)(4,1)} %get-tuple-element.43) | copy-start | bytes 196
  56.2 30.4 %copy-start.6 = (bf16[1,2048,4,128]{3,2,1,0:T(4,128)(2,1)S(1)}, bf16[1,2048,4,128]{3,2,1,0:T(4,128)(2,1)}, u32[]{:S(2)}) copy-start(bf16[1,2048,4,128]{3,2,1,0:T(4,128)(2,1)} %get-tuple-element.18) | copy-start | bytes 6291460
  86.6 4.4 %copy-start.2 = (f32[4,16,8,2048]{3,2,1,0:T(8,128)S(1)}, f32[4,16,8,2048]{3,2,1,0:T(8,128)}, u32[]{:S(2)}) copy-start(f32[4,16,8,2048]{3,2,1,0:T(8,128)} %get-tuple-element.68) | copy-start | bytes 12582916
  91.0 2.2 %copy-start.4 = (f32[4,16,8,2048]{3,2,1,0:T(8,128)S(1)}, f32[4,16,8,2048]{3,2,1,0:T(8,128)}, u32[]{:S(2)}) copy-start(f32[4,16,8,2048]{3,2,1,0:T(8,128)} %get-tuple-element.72) | copy-start | bytes 12582916
  93.2 2.2 %copy-start = (f32[4,16,8,2048]{3,2,1,0:T(8,128)S(1)}, f32[4,16,8,2048]{3,2,1,0:T(8,128)}, u32[]{:S(2)}) copy-start(f32[4,16,8,2048]{3,2,1,0:T(8,128)} %get-tuple-element.76) | copy-start | bytes 12582916
  97.7 3.5 %copy-start.3 = (f32[4,16,8,2048]{3,2,1,0:T(8,128)S(1)}, f32[4,16,8,2048]{3,2,1,0:T(8,128)}, u32[]{:S(2)}) copy-start(f32[4,16,8,2048]{3,2,1,0:T(8,128)} %get-tuple-element.68) | copy-start | bytes 12582916
  97.7 4.9 %copy-start.5 = (f32[4,16,8,2048]{3,2,1,0:T(8,128)S(1)}, f32[4,16,8,2048]{3,2,1,0:T(8,128)}, u32[]{:S(2)}) copy-start(f32[4,16,8,2048]{3,2,1,0:T(8,128)} %get-tuple-element.72) | copy-start | bytes 12582916
  101.1 2.8 %copy-start.1 = (f32[4,16,8,2048]{3,2,1,0:T(8,128)S(1)}, f32[4,16,8,2048]{3,2,1,0:T(8,128)}, u32[]{:S(2)}) copy-start(f32[4,16,8,2048]{3,2,1,0:T(8,128)} %get-tuple-element.76) | copy-start | bytes 12582916
Sparse Core Ops, SparseCore 0:
  97.8 53.5 all-reduce.4
where the time goes:
time: 164 us
  blocking collectives  67.7 us (41%)
  matrix products  27.9 us (17%)
  waiting for transfers between devices  25.2 us (15%)
  other arithmetic  17.6 us (11%)
  between operations  13.9 us (8%)
  local copies, waits for them, and re-layouts  11.3 us (7%)
    psum x1, waiting for transfers between devices, attend(): total_all, numerator_all = lax.psum((totals, numerator), 'ctx')  25.2 us
    all_gather x4, blocking collectives, resample_whole(): lax.all_gather(flat_rows, 'dom', axis=1, tiled=True)  24.2 us
    pmax x1, blocking collectives, attend(): peak_score = lax.pmax(local_peak, 'ctx')  22.2 us
    psum x1, blocking collectives, attend(): total_all, numerator_all = lax.psum((totals, numerator), 'ctx')  21.4 us
    dot_general x4, matrix products, attend(): jnp.einsum('pkgh,tkh->kpgt', query_block, prompt_keys, preferred_element_...  13.4 us
    dot_general x4, matrix products, attend(): jnp.einsum('kpgt,tkh->pkgh', prompt_weights, prompt_values, preferred_ele...  6.59 us
    reduce_sum x4, other arithmetic, attend(): jnp.sum(prompt_exp, axis=-1)  5.62 us
    another operation x5, other arithmetic, on_device(): return jnp.stack(results)  4.42 us
  transfers between devices with their start and end apart: 1, of which 1 were waited for; matrix products, arithmetic and copies ran while one was open for 3% of the time, Pallas kernels for 0%

commit v1 on v0

v1 whole, which is shorter than its diff:
```python
import functools
import math

import jax
import jax.numpy as jnp
from jax import lax
from jax.experimental import pallas as pl
from jax.experimental.pallas import tpu as pltpu
from jax.sharding import PartitionSpec as P

MESH = pl.DeviceIdType.MESH
SG = 2
D_LOCAL, D_MERGE, D_SPREAD = 1, 2, 4
F32, BF16 = jnp.float32, jnp.bfloat16


def log2_int(n):
    assert n & (n - 1) == 0
    return n.bit_length() - 1


def nt(a, b):
    return lax.dot_general(a, b, (((1,), (1,)), ((), ())), preferred_element_type=F32)


def nn(a, b):
    return jnp.dot(a, b, preferred_element_type=F32)


def iota(shape, dim):
    return lax.broadcasted_iota(jnp.int32, shape, dim)


def kernel(
    n_ctx, owners, suf_dev, score_mul,
    q_ref, prompt_hbm, suf_hbm, new_hbm, anc_ref, len_ref, out_ref,
    raw, kf, vf, kh, vth, s_scr,
    suf_g, new_g, sfk, sfv, nfk, nfv, mask,
    acc, stat, msg, got_l, got_r, gst_l, gst_r,
    load_sem, ex_local, ex_send, ex_recv,
    rs_send, rs_recv_l, rs_recv_r, ag_send_l, ag_send_r, ag_recv,
):
    steps, per, heads, group, hd = q_ref.shape
    particles = per * owners
    prompt = kh.shape[0]
    rows = SG * per * group
    groups_of_steps = steps // SG
    nb = heads * groups_of_steps
    lo, hi = n_ctx // 2 - 1, n_ctx // 2
    z = lax.axis_index("ctx")
    me = lax.axis_index("dom")
    n_suf = particles * suf_dev
    shares = n_ctx // steps
    chunk = per // shares
    n_new = owners * chunk
    n_ext = mask.shape[1]
    my_step = z // shares
    p0 = lax.rem(z, shares) * chunk

    loads = [
        pltpu.make_async_copy(prompt_hbm.at[i], raw.at[i], load_sem.at[i]) for i in range(2)
    ]
    for c in loads:
        c.start()

    barrier = pltpu.get_barrier_semaphore()
    for d in range(1, owners):
        pl.semaphore_signal(
            barrier, inc=1, device_id={"dom": lax.rem(me + d, owners)}, device_id_type=MESH
        )

    @pl.when(z > 0)
    def _():
        pl.semaphore_signal(barrier, inc=1, device_id={"ctx": z - 1}, device_id_type=MESH)

    @pl.when(z < n_ctx - 1)
    def _():
        pl.semaphore_signal(barrier, inc=1, device_id={"ctx": z + 1}, device_id_type=MESH)

    expected = (owners - 1) + jnp.where(z > 0, 1, 0) + jnp.where(z < n_ctx - 1, 1, 0)
    pl.semaphore_wait(barrier, expected)

    if shares == 1:
        new_src = new_hbm.at[my_step]
    else:
        new_src = new_hbm.at[
            my_step, :, pl.ds(pl.multiple_of(p0 * heads, chunk * heads), chunk * heads), :
        ]
    exchange = []
    for d in range(1, owners):
        peer = {"dom": lax.rem(me + d, owners)}
        for i, (src, dst) in enumerate(((suf_hbm, suf_g), (new_src, new_g))):
            exchange.append(
                pltpu.make_async_remote_copy(
                    src_ref=src, dst_ref=dst.at[me],
                    send_sem=ex_send.at[i, d - 1], recv_sem=ex_recv.at[i, d - 1],
                    device_id=peer, device_id_type=MESH,
                )
            )
    own = [
        pltpu.make_async_copy(suf_hbm, suf_g.at[me], ex_local.at[0]),
        pltpu.make_async_copy(new_src, new_g.at[me], ex_local.at[1]),
    ]
    for c in exchange + own:
        c.start()

    key = iota((n_ext, particles), 0)
    col = iota((n_ext, particles), 1)
    suf_particle = key >> log2_int(suf_dev)
    suf_pos = (key & (suf_dev - 1)) + z * suf_dev
    reach = (key < n_suf) & (suf_particle == col) & (suf_pos < len_ref[...])
    state = jnp.where(reach, 1.0, 0.0)
    rest = key - n_suf
    new_particle = (rest >> log2_int(chunk)) * per + (rest & (chunk - 1)) + p0
    is_new = jnp.where(
        (rest >= 0) & (rest < n_new) & (new_particle == col), 1.0, 0.0
    )
    spread = jnp.where(
        iota((particles, per * group), 0)
        == (iota((particles, per * group), 1) >> log2_int(group)) + me * per,
        1.0, 0.0,
    ).astype(BF16)
    for s in range(steps):
        parents = anc_ref[pl.ds(s, 1), :]
        move = jnp.where(iota((particles, particles), 0) == parents, 1.0, 0.0).astype(BF16)
        state = nn(state.astype(BF16), move)
        state = state + is_new * jnp.where(my_step == s, 1.0, 0.0)
        wide = nn(state.astype(BF16), spread)
        mask[s] = jnp.where(wide > 0.5, 0.0, -1e30)

    for src, dst in ((0, kf), (1, vf)):
        loads[src].wait()
        size = 1024

        def widen(i, _, src=src, dst=dst):
            at = pl.ds(pl.multiple_of(i * size, size), size)
            dst[at, :] = raw[src, at, :].astype(F32)
            return 0

        lax.fori_loop(0, raw.shape[1] // size, widen, 0)

    def parts(b):
        h = b // groups_of_steps
        return h, (b - h * groups_of_steps) * SG

    def queries_of(b):
        h, s0 = parts(b)
        out = [
            q_ref[s0 + i, :, h].astype(F32).reshape(per * group, hd) for i in range(SG)
        ]
        return jnp.concatenate(out, axis=0).astype(BF16)

    def prompt_stage(b):
        h, s0 = parts(b)

        @pl.when(s0 == 0)
        def _():
            size = 256
            for i in range(prompt // size):
                at = pl.ds(h + i * size * heads, size, stride=heads)
                kh[pl.ds(i * size, size), :] = kf[at, :].astype(BF16)
                vth[:, pl.ds(i * size, size)] = vf[at, :].T.astype(BF16)

        q = queries_of(b)
        size = 512
        top = None
        for i in range(prompt // size):
            at = pl.ds(i * size, size)
            s = nt(kh[at, :], q)
            s_scr[at, :] = s
            t = jnp.max(s, axis=0, keepdims=True)
            top = t if top is None else jnp.maximum(top, t)
        top = top * score_mul
        total = jnp.zeros((1, rows), F32)
        numer = jnp.zeros((hd, rows), F32)
        for i in range(prompt // size):
            at = pl.ds(i * size, size)
            w = jnp.exp2(s_scr[at, :] * score_mul - top)
            total += jnp.sum(w, axis=0, keepdims=True)
            numer += nn(vth[:, at], w.astype(BF16))
        acc[b] = numer
        put_stat(b, top, total)

    def put_stat(b, top, total):
        stat[b] = jnp.where(iota((8, rows), 0) == 0, top, total)

    def merge(first, second):
        m1, l1, a1 = first
        m2, l2, a2 = second
        m = jnp.maximum(m1, m2)
        c1, c2 = jnp.exp2(m1 - m), jnp.exp2(m2 - m)
        return m, l1 * c1 + l2 * c2, a1 * c1 + a2 * c2

    def held(b):
        return stat[b, 0:1, :], stat[b, 1:2, :], acc[b]

    def rs_copies(b, right):
        data, small = (got_l, gst_l) if right else (got_r, gst_r)
        sems = rs_recv_l if right else rs_recv_r
        peer = {"ctx": z + 1} if right else {"ctx": z - 1}
        return [
            pltpu.make_async_remote_copy(
                src_ref=src.at[b], dst_ref=dst.at[b],
                send_sem=rs_send.at[i, b], recv_sem=sems.at[i, b],
                device_id=peer, device_id_type=MESH,
            )
            for i, (src, dst) in enumerate(((stat, small), (msg, data)))
        ]

    def owner_of(b):
        return jnp.where(lax.rem(b, 2) == 0, lo, hi)

    def send_partial(b):
        @pl.when(z < owner_of(b))
        def _():
            for c in rs_copies(b, True):
                c.start()

        @pl.when(z > owner_of(b))
        def _():
            for c in rs_copies(b, False):
                c.start()

    def unpack_extra():
        for c in own:
            c.wait()
        for c in exchange:
            c.wait()
        ps, pn = suf_g.shape[2], new_g.shape[2]
        for o in range(owners):
            for i, dst in enumerate((sfk, sfv)):
                dst[pl.ds(o * ps, ps), :] = suf_g[o, i].astype(F32)
            for i, dst in enumerate((nfk, nfv)):
                dst[pl.ds(o * pn, pn), :] = new_g[o, i].astype(F32)

    def local_stage(b):
        @pl.when(b == 0)
        def _():
            unpack_extra()

        h, s0 = parts(b)
        pad = jnp.zeros((n_ext - n_suf - n_new, hd), F32)

        def rows_of(suf, new):
            pieces = [suf[pl.ds(h, n_suf, stride=heads), :], new[pl.ds(h, n_new, stride=heads), :]]
            return jnp.concatenate(pieces + ([pad] if pad.shape[0] else []), axis=0)

        ks = rows_of(sfk, nfk).astype(BF16)
        vt = rows_of(sfv, nfv).T.astype(BF16)
        bias = jnp.concatenate([mask[s0 + i] for i in range(SG)], axis=1)
        s = nt(ks, queries_of(b)) * score_mul + bias
        top = jnp.max(s, axis=0, keepdims=True)
        old_top, old_total, old_numer = held(b)
        new_top = jnp.maximum(old_top, top)
        w = jnp.exp2(s - new_top)
        keep = jnp.exp2(old_top - new_top)
        total = old_total * keep + jnp.sum(w, axis=0, keepdims=True)
        numer = old_numer * keep + nn(vt, w.astype(BF16))
        put_stat(b, new_top, total)
        acc[b] = numer
        msg[b] = numer.astype(BF16)

        @pl.when((z == 0) | (z == n_ctx - 1))
        def _():
            @pl.when(z != owner_of(b))
            def _():
                send_partial(b)

    def recv_partial(b, from_left):
        data, small = (got_l, gst_l) if from_left else (got_r, gst_r)
        for c in rs_copies(b, from_left):
            c.wait_recv()
        top, total, numer = merge(
            held(b), (small[b, 0:1, :], small[b, 1:2, :], data[b].astype(F32))
        )
        put_stat(b, top, total)
        acc[b] = numer

    def ag_copy(b, right, i):
        h, s0 = parts(b)
        at = out_ref.at[s0 + i, :, h]
        sems = ag_send_r if right else ag_send_l
        return pltpu.make_async_remote_copy(
            src_ref=at, dst_ref=at,
            send_sem=sems.at[i, b], recv_sem=ag_recv.at[i, b],
            device_id={"ctx": z + 1} if right else {"ctx": z - 1}, device_id_type=MESH,
        )

    def ag_send(b):
        for i in range(SG):
            @pl.when((z <= owner_of(b)) & (z > 0))
            def _():
                ag_copy(b, False, i).start()

            @pl.when((z >= owner_of(b)) & (z < n_ctx - 1))
            def _():
                ag_copy(b, True, i).start()

    def merge_stage(b):
        owner = owner_of(b)

        @pl.when((z > 0) & (z <= owner))
        def _():
            recv_partial(b, True)

        @pl.when((z < n_ctx - 1) & (z >= owner))
        def _():
            recv_partial(b, False)

        @pl.when((z != owner) & (z > 0) & (z < n_ctx - 1))
        def _():
            msg[b] = acc[b].astype(BF16)
            send_partial(b)

        @pl.when(z == owner)
        def _():
            _, total, numer = held(b)
            h, s0 = parts(b)
            done = numer / total
            for i in range(SG):
                wide = done[:, i * per * group:(i + 1) * per * group].T
                out_ref[s0 + i, :, h] = wide.reshape(per, group, hd).astype(BF16)
            ag_send(b)

    def spread_stage(b):
        owner = owner_of(b)

        @pl.when(z != owner)
        def _():
            for i in range(SG):
                ag_copy(b, True, i).wait_recv()
            ag_send(b)

    def finish(b):
        owner = owner_of(b)

        @pl.when(z != owner)
        def _():
            for c in rs_copies(b, True):
                c.wait_send()

        for i in range(SG):
            @pl.when((z <= owner) & (z > 0))
            def _():
                ag_copy(b, False, i).wait_send()

            @pl.when((z >= owner) & (z < n_ctx - 1))
            def _():
                ag_copy(b, True, i).wait_send()

    def run(i, _):
        for delay, stage in (
            (0, prompt_stage), (D_LOCAL, local_stage), (D_MERGE, merge_stage), (D_SPREAD, spread_stage)
        ):
            @pl.when((i >= delay) & (i < nb + delay))
            def _(delay=delay, stage=stage):
                stage(i - delay)
        return 0

    lax.fori_loop(0, nb + D_SPREAD, run, 0)

    def close(b, _):
        finish(b)
        return 0

    lax.fori_loop(0, nb, close, 0)


def on_device(n_ctx, owners, queries, prompt_cache, suffix_cache, new_kv, ancestors, lengths):
    steps, per, heads, group, hd = queries.shape
    prompt = prompt_cache.shape[1]
    suf_dev = suffix_cache.shape[2]
    particles = ancestors.shape[1]
    rows = SG * per * group
    nb = heads * (steps // SG)
    shares = n_ctx // steps
    chunk = per // shares
    n_ext = -(-(particles * suf_dev + owners * chunk) // 128) * 128
    dma = pltpu.SemaphoreType.DMA
    score_mul = math.log2(math.e) / math.sqrt(hd)
    ps, pn = per * suf_dev * heads, chunk * heads
    any_spec = pl.BlockSpec(memory_space=pl.ANY)
    vmem_spec = pl.BlockSpec(memory_space=pltpu.VMEM)
    return pl.pallas_call(
        functools.partial(kernel, n_ctx, owners, suf_dev, score_mul),
        out_shape=jax.ShapeDtypeStruct(queries.shape, BF16),
        in_specs=[vmem_spec, any_spec, any_spec, any_spec, vmem_spec, vmem_spec],
        out_specs=vmem_spec,
        scratch_shapes=[
            pltpu.VMEM((2, prompt * heads, hd), BF16),
            pltpu.VMEM((prompt * heads, hd), F32),
            pltpu.VMEM((prompt * heads, hd), F32),
            pltpu.VMEM((prompt, hd), BF16),
            pltpu.VMEM((hd, prompt), BF16),
            pltpu.VMEM((prompt, rows), F32),
            pltpu.VMEM((owners, 2, ps, hd), BF16),
            pltpu.VMEM((owners, 2, pn, hd), BF16),
            pltpu.VMEM((owners * ps, hd), F32),
            pltpu.VMEM((owners * ps, hd), F32),
            pltpu.VMEM((owners * pn, hd), F32),
            pltpu.VMEM((owners * pn, hd), F32),
            pltpu.VMEM((steps, n_ext, per * group), F32),
            pltpu.VMEM((nb, hd, rows), F32),
            pltpu.VMEM((nb, 8, rows), F32),
            pltpu.VMEM((nb, hd, rows), BF16),
            pltpu.VMEM((nb, hd, rows), BF16),
            pltpu.VMEM((nb, hd, rows), BF16),
            pltpu.VMEM((nb, 8, rows), F32),
            pltpu.VMEM((nb, 8, rows), F32),
            dma((2,)),
            dma((2,)),
            dma((2, max(owners - 1, 1))),
            dma((2, max(owners - 1, 1))),
            dma((2, nb)),
            dma((2, nb)),
            dma((2, nb)),
            dma((SG, nb)),
            dma((SG, nb)),
            dma((SG, nb)),
        ],
        compiler_params=pltpu.CompilerParams(
            collective_id=0, has_side_effects=True, vmem_limit_bytes=60 << 20
        ),
    )(
        queries,
        prompt_cache.reshape(2, prompt * heads, hd),
        suffix_cache.reshape(2, ps, hd),
        new_kv.reshape(steps, 2, per * heads, hd),
        ancestors,
        lengths.reshape(1, particles),
    )


def solution(mesh):
    return jax.shard_map(
        functools.partial(on_device, mesh.shape["ctx"], mesh.shape["dom"]),
        mesh=mesh,
        in_specs=(
            P("groups", "dom", "tp", None, None),
            P("groups", "ctx", "tp", None),
            P("groups", "dom", "ctx", "tp", None),
            P("groups", None, "dom", "tp", None),
            P("groups", None),
            P("groups"),
        ),
        out_specs=P("groups", "dom", "tp", None, None),
        check_vma=False,
    )
```

time: 164 us -> 65.1 us (0.40)
  blocking collectives: 67.7 us -> 0 us
  Pallas kernels: 0 us -> 63.1 us
  matrix products: 27.9 us -> 0 us
  waiting for transfers between devices: 25.2 us -> 0 us
  other arithmetic: 17.6 us -> 0 us
  between operations: 13.9 us -> 0.01 us
  local copies, waits for them, and re-layouts: 11.3 us -> 1.87 us
    pallas_call x0 -> x1, Pallas kernels: none -> 63.1 us  [on_device(): pl.pallas_call(functools.partial(kernel, n_ctx, owners, suf_dev, score_mu...]
    dot_general x20 -> x0, matrix products: 27.9 us -> none  [the longest x4 13.4 us: attend(): jnp.einsum('pkgh,tkh->kpgt', query_block, prompt_keys, preferred_element_...]
    psum x1 -> x0, waiting for transfers between devices: 25.2 us -> none  [attend(): total_all, numerator_all = lax.psum((totals, numerator), 'ctx')]
    all_gather x4 -> x0, blocking collectives: 24.2 us -> none  [resample_whole(): lax.all_gather(flat_rows, 'dom', axis=1, tiled=True)]
    pmax x1 -> x0, blocking collectives: 22.2 us -> none  [attend(): peak_score = lax.pmax(local_peak, 'ctx')]
    psum x1 -> x0, blocking collectives: 21.4 us -> none  [attend(): total_all, numerator_all = lax.psum((totals, numerator), 'ctx')]
    reduce_sum x12 -> x0, other arithmetic: 8.47 us -> none  [the longest x4 5.62 us: attend(): jnp.sum(prompt_exp, axis=-1)]
    slice x2 -> x0, local copies, waits for them, and re-layouts: 4.89 us -> none  [the longest x1 4.11 us: on_device(): prompt_keys = prompt_cache[0]]
  transfers between devices with their start and end apart: 1 -> 0, of which waited for: 1 -> 0; matrix products, arithmetic and copies ran while one was open for 3% -> 0% of each run, Pallas kernels for 0% -> 0%
where the time goes in v1:
time: 65.1 us; the launch traced here: 65 us
  Pallas kernels  63.1 us (97%)
  local copies, waits for them, and re-layouts  1.87 us (3%)
    pallas_call x1, Pallas kernels, on_device(): pl.pallas_call(functools.partial(kernel, n_ctx, owners, suf_dev, score_mu...  63.1 us
    unnamed x1, local copies, waits for them, and re-layouts  1.87 us

profile of v1, /device:TPU:0, one launch (start us, length us, event | category | flops | bytes accessed | tf_op | source)
XLA Modules:
  0.0 65.0 jit_solution(1445561149973156045)
XLA Ops:
  0.0 63.1 %shard_map.64 = bf16[4,16,4,8,128]{4,3,2,1,0:T(8,128)(2,1)} custom-call(bf16[4,16,4,8,128]{4,3,2,1,0:T(8,128)(2,1)} %q_ref.1, bf16[2,8192,128]{2,1,0:T(8,128)(2,1)} %bitcast.4, bf16[2,256,128]{2,1,0:T(8,128)(2,1)} %bitcast.5, bf16[4,2,64,128]{3,2,1,0:T(8,128)(2,1)} %bitcast.6, s32[4,32]{1,0:T(4,128)} %anc_ref.1, s32[1,32]{1,0:T(1,128)} %bitcast.7), custom_call_target="tpu_custom_call" | custom-call | tf_op jit(solution)/shard_map/pallas_call | solution.py:384
  63.1 1.9 %copy.8 = bf16[4,16,4,8,128]{4,3,2,1,0:T(8,128)(2,1)} copy(bf16[4,16,4,8,128]{4,3,2,1,0:T(8,128)(2,1)} %shard_map.64) | data formatting | bytes 1048576

commit v2 on v1

v2 whole, which is shorter than its diff:
```python
import functools
import math

import jax
import jax.numpy as jnp
from jax import lax
from jax.experimental import pallas as pl
from jax.experimental.pallas import tpu as pltpu
from jax.sharding import PartitionSpec as P

MESH = pl.DeviceIdType.MESH
SG = 2
CS = 1
AHEAD = 4
D_FOLD, D_SWAP = 5, 7
F32, BF16 = jnp.float32, jnp.bfloat16


def log2_int(n):
    assert n & (n - 1) == 0
    return n.bit_length() - 1


def nt(a, b):
    return lax.dot_general(a, b, (((1,), (1,)), ((), ())), preferred_element_type=F32)


def nn(a, b):
    return jnp.dot(a, b, preferred_element_type=F32)


def iota(shape, dim):
    return lax.broadcasted_iota(jnp.int32, shape, dim)


def kernel(
    n_ctx, owners, suf_dev, score_mul,
    q_ref, prompt_hbm, suf_hbm, new_hbm, anc_ref, len_ref, out_ref,
    raw, kf, vf, kh, vth, kx, vx, s_scr,
    suf_g, new_g, sfk, sfv, nfk, nfv, mask,
    acc, stat, msg, got_out, got_in, gst_out, gst_in, fin,
    load_sem, ex_local, ex_send, ex_recv,
    rs_send, rs_recv_out, rs_recv_in, ag_send, ag_recv,
):
    steps, per, heads, group, hd = q_ref.shape
    particles = per * owners
    prompt = kh.shape[0]
    rows = SG * per * group
    groups_of_steps = steps // SG
    nb = heads * groups_of_steps
    cuts = SG // CS
    width = CS * per * group
    lo, hi = n_ctx // 2 - 1, n_ctx // 2
    z = lax.axis_index("ctx")
    me = lax.axis_index("dom")
    n_suf = particles * suf_dev
    shares = n_ctx // steps
    chunk = per // shares
    n_new = owners * chunk
    n_ext = mask.shape[1]
    my_step = z // shares
    p0 = lax.rem(z, shares) * chunk

    loads = [
        pltpu.make_async_copy(prompt_hbm.at[i], raw.at[i], load_sem.at[i]) for i in range(2)
    ]
    for c in loads:
        c.start()

    barrier = pltpu.get_barrier_semaphore()
    for d in range(1, owners):
        pl.semaphore_signal(
            barrier, inc=1, device_id={"dom": lax.rem(me + d, owners)}, device_id_type=MESH
        )

    @pl.when(z > 0)
    def _():
        pl.semaphore_signal(barrier, inc=1, device_id={"ctx": z - 1}, device_id_type=MESH)

    @pl.when(z < n_ctx - 1)
    def _():
        pl.semaphore_signal(barrier, inc=1, device_id={"ctx": z + 1}, device_id_type=MESH)

    expected = (owners - 1) + jnp.where(z > 0, 1, 0) + jnp.where(z < n_ctx - 1, 1, 0)
    pl.semaphore_wait(barrier, expected)

    if shares == 1:
        new_src = new_hbm.at[my_step]
    else:
        new_src = new_hbm.at[
            my_step, :, pl.ds(pl.multiple_of(p0 * heads, chunk * heads), chunk * heads), :
        ]
    exchange = []
    for d in range(1, owners):
        peer = {"dom": lax.rem(me + d, owners)}
        for i, (src, dst) in enumerate(((suf_hbm, suf_g), (new_src, new_g))):
            exchange.append(
                pltpu.make_async_remote_copy(
                    src_ref=src, dst_ref=dst.at[me],
                    send_sem=ex_send.at[i, d - 1], recv_sem=ex_recv.at[i, d - 1],
                    device_id=peer, device_id_type=MESH,
                )
            )
    own = [
        pltpu.make_async_copy(suf_hbm, suf_g.at[me], ex_local.at[0]),
        pltpu.make_async_copy(new_src, new_g.at[me], ex_local.at[1]),
    ]
    for c in exchange + own:
        c.start()

    key = iota((n_ext, particles), 0)
    col = iota((n_ext, particles), 1)
    suf_particle = key >> log2_int(suf_dev)
    suf_pos = (key & (suf_dev - 1)) + z * suf_dev
    reach = (key < n_suf) & (suf_particle == col) & (suf_pos < len_ref[...])
    state = jnp.where(reach, 1.0, 0.0)
    rest = key - n_suf
    new_particle = (rest >> log2_int(chunk)) * per + (rest & (chunk - 1)) + p0
    is_new = jnp.where(
        (rest >= 0) & (rest < n_new) & (new_particle == col), 1.0, 0.0
    )
    spread = jnp.where(
        iota((particles, per * group), 0)
        == (iota((particles, per * group), 1) >> log2_int(group)) + me * per,
        1.0, 0.0,
    ).astype(BF16)
    for s in range(steps):
        parents = anc_ref[pl.ds(s, 1), :]
        move = jnp.where(iota((particles, particles), 0) == parents, 1.0, 0.0).astype(BF16)
        state = nn(state.astype(BF16), move)
        state = state + is_new * jnp.where(my_step == s, 1.0, 0.0)
        wide = nn(state.astype(BF16), spread)
        mask[s] = jnp.where(wide > 0.5, 0.0, -1e30)

    for src, dst in ((0, kf), (1, vf)):
        loads[src].wait()
        size = 1024

        def widen(i, _, src=src, dst=dst):
            at = pl.ds(pl.multiple_of(i * size, size), size)
            dst[at, :] = raw[src, at, :].astype(F32)
            return 0

        lax.fori_loop(0, raw.shape[1] // size, widen, 0)

    def parts(b):
        h = b // groups_of_steps
        return h, (b - h * groups_of_steps) * SG

    def queries_of(b):
        h, s0 = parts(b)
        out = [
            q_ref[s0 + i, :, h].astype(F32).reshape(per * group, hd) for i in range(SG)
        ]
        return jnp.concatenate(out, axis=0).astype(BF16)

    def extra_rows(suf, new, h):
        pieces = [suf[pl.ds(h, n_suf, stride=heads), :], new[pl.ds(h, n_new, stride=heads), :]]
        if n_ext > n_suf + n_new:
            pieces.append(jnp.zeros((n_ext - n_suf - n_new, hd), F32))
        return jnp.concatenate(pieces, axis=0)

    def bias_of(s0):
        return jnp.concatenate([mask[s0 + i] for i in range(SG)], axis=1)

    def prompt_stage(b, extra):
        h, s0 = parts(b)

        @pl.when(s0 == 0)
        def _():
            size = 256
            for i in range(prompt // size):
                at = pl.ds(h + i * size * heads, size, stride=heads)
                kh[pl.ds(i * size, size), :] = kf[at, :].astype(BF16)
                vth[:, pl.ds(i * size, size)] = vf[at, :].T.astype(BF16)
            if extra:
                kx[...] = extra_rows(sfk, nfk, h).astype(BF16)
                vx[...] = extra_rows(sfv, nfv, h).T.astype(BF16)

        q = queries_of(b)
        size = 512
        top = None
        if extra:
            sx = nt(kx[...], q) * score_mul + bias_of(s0)
        for i in range(prompt // size):
            at = pl.ds(i * size, size)
            s = nt(kh[at, :], q)
            s_scr[at, :] = s
            t = jnp.max(s, axis=0, keepdims=True)
            top = t if top is None else jnp.maximum(top, t)
        top = top * score_mul
        total = jnp.zeros((1, rows), F32)
        numer = jnp.zeros((hd, rows), F32)
        if extra:
            top = jnp.maximum(top, jnp.max(sx, axis=0, keepdims=True))
            w = jnp.exp2(sx - top)
            total += jnp.sum(w, axis=0, keepdims=True)
            numer += nn(vx[...], w.astype(BF16))
        for i in range(prompt // size):
            at = pl.ds(i * size, size)
            w = jnp.exp2(s_scr[at, :] * score_mul - top)
            total += jnp.sum(w, axis=0, keepdims=True)
            numer += nn(vth[:, at], w.astype(BF16))
        put(b, top, total, numer, extra)
        if extra:
            start_inward(b)

    def put(b, top, total, numer, ready):
        small = jnp.where(iota((8, rows), 0) == 0, top, total)
        for i in range(cuts):
            at = slice(i * width, (i + 1) * width)
            stat[b * cuts + i] = small[:, at]
            acc[b * cuts + i] = numer[:, at]
            if ready:
                msg[b * cuts + i] = numer[:, at].astype(BF16)

    def unpack_extra():
        for c in own:
            c.wait()
        for c in exchange:
            c.wait()
        ps, pn = suf_g.shape[2], new_g.shape[2]
        for o in range(owners):
            for i, dst in enumerate((sfk, sfv)):
                dst[pl.ds(o * ps, ps), :] = suf_g[o, i].astype(F32)
            for i, dst in enumerate((nfk, nfv)):
                dst[pl.ds(o * pn, pn), :] = new_g[o, i].astype(F32)

    def local_stage(b):
        h, s0 = parts(b)
        ks = extra_rows(sfk, nfk, h).astype(BF16)
        vt = extra_rows(sfv, nfv, h).T.astype(BF16)
        s = nt(ks, queries_of(b)) * score_mul + bias_of(s0)
        small = jnp.concatenate([stat[b * cuts + i] for i in range(cuts)], axis=1)
        old_numer = jnp.concatenate([acc[b * cuts + i] for i in range(cuts)], axis=1)
        old_top, old_total = small[0:1], small[1:2]
        new_top = jnp.maximum(old_top, jnp.max(s, axis=0, keepdims=True))
        w = jnp.exp2(s - new_top)
        keep = jnp.exp2(old_top - new_top)
        total = old_total * keep + jnp.sum(w, axis=0, keepdims=True)
        numer = old_numer * keep + nn(vt, w.astype(BF16))
        put(b, new_top, total, numer, True)
        start_inward(b)

    mid = (z == lo) | (z == hi)
    left_half = z <= lo
    inner = jnp.where(left_half, z + 1, z - 1)
    outer = jnp.where(left_half, z - 1, z + 1)
    has_outer = (z > 0) & (z < n_ctx - 1)

    def inward(c, across):
        data, small, sems = (
            (got_in, gst_in, rs_recv_in) if across else (got_out, gst_out, rs_recv_out)
        )
        return [
            pltpu.make_async_remote_copy(
                src_ref=src.at[c], dst_ref=dst.at[c],
                send_sem=rs_send.at[i, c], recv_sem=sems.at[i, c],
                device_id={"ctx": inner}, device_id_type=MESH,
            )
            for i, (src, dst) in enumerate(((stat, small), (msg, data)))
        ]

    def outward(c):
        return pltpu.make_async_remote_copy(
            src_ref=fin.at[c], dst_ref=fin.at[c],
            send_sem=ag_send.at[c], recv_sem=ag_recv.at[c],
            device_id={"ctx": outer}, device_id_type=MESH,
        )

    def start_inward(b):
        @pl.when(jnp.logical_not(has_outer))
        def _():
            for i in range(cuts):
                send(b * cuts + i)

    def send(c):
        for across in (True, False):
            @pl.when(mid if across else jnp.logical_not(mid))
            def _(across=across):
                for copy in inward(c, across):
                    copy.start()

    def merge(first, second):
        m1, l1, a1 = first
        m2, l2, a2 = second
        m = jnp.maximum(m1, m2)
        c1, c2 = jnp.exp2(m1 - m), jnp.exp2(m2 - m)
        return m, l1 * c1 + l2 * c2, a1 * c1 + a2 * c2

    def fold_stage(c):
        @pl.when(has_outer)
        def _():
            for copy in inward(c, False):
                copy.wait_recv()
            top, total, numer = merge(
                (stat[c, 0:1, :], stat[c, 1:2, :], acc[c]),
                (gst_out[c, 0:1, :], gst_out[c, 1:2, :], got_out[c].astype(F32)),
            )
            stat[c] = jnp.where(iota((8, width), 0) == 0, top, total)
            msg[c] = numer.astype(BF16)
            send(c)

    def put_out(c):
        h = c // (groups_of_steps * cuts)
        s0 = (c - h * (groups_of_steps * cuts)) * CS
        for i in range(CS):
            out_ref[s0 + i, :, h] = fin[c, i]

    def swap_stage(c):
        @pl.when(mid)
        def _():
            for copy in inward(c, True):
                copy.wait_recv()
            mine = (stat[c], msg[c].astype(F32))
            theirs = (gst_in[c], got_in[c].astype(F32))
            low = [jnp.where(left_half, a, b) for a, b in zip(mine, theirs)]
            high = [jnp.where(left_half, b, a) for a, b in zip(mine, theirs)]
            _, total, numer = merge(
                (low[0][0:1], low[0][1:2], low[1]), (high[0][0:1], high[0][1:2], high[1])
            )
            done = numer / total
            for i in range(CS):
                wide = done[:, i * per * group:(i + 1) * per * group].T
                fin[c, i] = wide.reshape(per, group, hd).astype(BF16)

            @pl.when(has_outer)
            def _():
                outward(c).start()

            put_out(c)

    def spread_stage(c):
        @pl.when(jnp.logical_not(mid))
        def _():
            outward(c).wait_recv()

            @pl.when(has_outer)
            def _():
                outward(c).start()

            put_out(c)

        for across in (True, False):
            @pl.when(mid if across else jnp.logical_not(mid))
            def _(across=across):
                for copy in inward(c, across):
                    copy.wait_send()

        @pl.when(has_outer)
        def _():
            outward(c).wait_send()

    def each(stage, b):
        for i in range(cuts):
            stage(b * cuts + i)

    def run(i, _):
        @pl.when(i < AHEAD)
        def _():
            prompt_stage(i, False)

        @pl.when(i == AHEAD)
        def _():
            unpack_extra()

            def add(b, _):
                local_stage(b)
                return 0

            lax.fori_loop(0, AHEAD, add, 0)

        @pl.when((i >= AHEAD) & (i < nb))
        def _():
            prompt_stage(i, True)

        for delay, stage in ((D_FOLD, fold_stage), (D_SWAP, swap_stage)):
            @pl.when((i >= delay) & (i < nb + delay))
            def _(delay=delay, stage=stage):
                each(stage, i - delay)
        return 0

    lax.fori_loop(0, nb + D_SWAP, run, 0)

    def close(c, _):
        spread_stage(c)
        return 0

    lax.fori_loop(0, nb * cuts, close, 0)


def on_device(n_ctx, owners, queries, prompt_cache, suffix_cache, new_kv, ancestors, lengths):
    steps, per, heads, group, hd = queries.shape
    prompt = prompt_cache.shape[1]
    suf_dev = suffix_cache.shape[2]
    particles = ancestors.shape[1]
    rows = SG * per * group
    nc = heads * (steps // CS)
    width = CS * per * group
    shares = n_ctx // steps
    chunk = per // shares
    n_ext = -(-(particles * suf_dev + owners * chunk) // 128) * 128
    dma = pltpu.SemaphoreType.DMA
    score_mul = math.log2(math.e) / math.sqrt(hd)
    ps, pn = per * suf_dev * heads, chunk * heads
    any_spec = pl.BlockSpec(memory_space=pl.ANY)
    vmem_spec = pl.BlockSpec(memory_space=pltpu.VMEM)
    return pl.pallas_call(
        functools.partial(kernel, n_ctx, owners, suf_dev, score_mul),
        out_shape=jax.ShapeDtypeStruct(queries.shape, BF16),
        in_specs=[vmem_spec, any_spec, any_spec, any_spec, vmem_spec, vmem_spec],
        out_specs=vmem_spec,
        scratch_shapes=[
            pltpu.VMEM((2, prompt * heads, hd), BF16),
            pltpu.VMEM((prompt * heads, hd), F32),
            pltpu.VMEM((prompt * heads, hd), F32),
            pltpu.VMEM((prompt, hd), BF16),
            pltpu.VMEM((hd, prompt), BF16),
            pltpu.VMEM((n_ext, hd), BF16),
            pltpu.VMEM((hd, n_ext), BF16),
            pltpu.VMEM((prompt, rows), F32),
            pltpu.VMEM((owners, 2, ps, hd), BF16),
            pltpu.VMEM((owners, 2, pn, hd), BF16),
            pltpu.VMEM((owners * ps, hd), F32),
            pltpu.VMEM((owners * ps, hd), F32),
            pltpu.VMEM((owners * pn, hd), F32),
            pltpu.VMEM((owners * pn, hd), F32),
            pltpu.VMEM((steps, n_ext, per * group), F32),
            pltpu.VMEM((nc, hd, width), F32),
            pltpu.VMEM((nc, 8, width), F32),
            pltpu.VMEM((nc, hd, width), BF16),
            pltpu.VMEM((nc, hd, width), BF16),
            pltpu.VMEM((nc, hd, width), BF16),
            pltpu.VMEM((nc, 8, width), F32),
            pltpu.VMEM((nc, 8, width), F32),
            pltpu.VMEM((nc, CS, per, group, hd), BF16),
            dma((2,)),
            dma((2,)),
            dma((2, max(owners - 1, 1))),
            dma((2, max(owners - 1, 1))),
            dma((2, nc)),
            dma((2, nc)),
            dma((2, nc)),
            dma((nc,)),
            dma((nc,)),
        ],
        compiler_params=pltpu.CompilerParams(
            collective_id=0, has_side_effects=True, vmem_limit_bytes=60 << 20
        ),
    )(
        queries,
        prompt_cache.reshape(2, prompt * heads, hd),
        suffix_cache.reshape(2, ps, hd),
        new_kv.reshape(steps, 2, per * heads, hd),
        ancestors,
        lengths.reshape(1, particles),
    )


def solution(mesh):
    return jax.shard_map(
        functools.partial(on_device, mesh.shape["ctx"], mesh.shape["dom"]),
        mesh=mesh,
        in_specs=(
            P("groups", "dom", "tp", None, None),
            P("groups", "ctx", "tp", None),
            P("groups", "dom", "ctx", "tp", None),
            P("groups", None, "dom", "tp", None),
            P("groups", None),
            P("groups"),
        ),
        out_specs=P("groups", "dom", "tp", None, None),
        check_vma=False,
    )
```

time: 65.1 us -> 38.2 us (0.59)
  Pallas kernels: 63.1 us -> 36.1 us
    pallas_call x1, Pallas kernels: 63.1 us -> 36.1 us  [on_device(): pl.pallas_call(functools.partial(kernel, n_ctx, owners, suf_dev, score_mu...]
where the time goes in v2:
time: 38.2 us; the launch traced here: 38 us
  Pallas kernels  36.1 us (95%)
  local copies, waits for them, and re-layouts  1.87 us (5%)
    pallas_call x1, Pallas kernels, on_device(): pl.pallas_call(functools.partial(kernel, n_ctx, owners, suf_dev, score_mu...  36.1 us
    unnamed x1, local copies, waits for them, and re-layouts  1.87 us

profile of v2, /device:TPU:0, one launch (start us, length us, event | category | flops | bytes accessed | tf_op | source)
XLA Modules:
  0.0 38.0 jit_solution(17687447939901122709)
XLA Ops:
  0.0 36.1 %shard_map.64 = bf16[4,16,4,8,128]{4,3,2,1,0:T(8,128)(2,1)} custom-call(bf16[4,16,4,8,128]{4,3,2,1,0:T(8,128)(2,1)} %q_ref.1, bf16[2,8192,128]{2,1,0:T(8,128)(2,1)} %bitcast.4, bf16[2,256,128]{2,1,0:T(8,128)(2,1)} %bitcast.5, bf16[4,2,64,128]{3,2,1,0:T(8,128)(2,1)} %bitcast.6, s32[4,32]{1,0:T(4,128)} %anc_ref.1, s32[1,32]{1,0:T(1,128)} %bitcast.7), custom_call_target="tpu_custom_call" | custom-call | tf_op jit(solution)/shard_map/pallas_call | solution.py:408
  36.1 1.9 %copy.8 = bf16[4,16,4,8,128]{4,3,2,1,0:T(8,128)(2,1)} copy(bf16[4,16,4,8,128]{4,3,2,1,0:T(8,128)(2,1)} %shard_map.64) | data formatting | bytes 1048576

commit v3 on v2

--- a/solution.py
+++ b/solution.py
@@ -10,9 +10,9 @@
 
 MESH = pl.DeviceIdType.MESH
 SG = 2
-CS = 1
-AHEAD = 4
-D_FOLD, D_SWAP = 5, 7
+CS = 2
+AHEAD = 2
+D_FOLD, D_SWAP = 2, 5
 F32, BF16 = jnp.float32, jnp.bfloat16
 
 
@@ -206,7 +206,7 @@
             start_inward(b)
 
     def put(b, top, total, numer, ready):
-        small = jnp.where(iota((8, rows), 0) == 0, top, total)
+        small = jnp.where(iota((2, rows), 0) == 0, top, total)
         for i in range(cuts):
             at = slice(i * width, (i + 1) * width)
             stat[b * cuts + i] = small[:, at]
@@ -297,7 +297,7 @@
                 (stat[c, 0:1, :], stat[c, 1:2, :], acc[c]),
                 (gst_out[c, 0:1, :], gst_out[c, 1:2, :], got_out[c].astype(F32)),
             )
-            stat[c] = jnp.where(iota((8, width), 0) == 0, top, total)
+            stat[c] = jnp.where(iota((2, width), 0) == 0, top, total)
             msg[c] = numer.astype(BF16)
             send(c)
 
@@ -427,12 +427,12 @@
             pltpu.VMEM((owners * pn, hd), F32),
             pltpu.VMEM((steps, n_ext, per * group), F32),
             pltpu.VMEM((nc, hd, width), F32),
-            pltpu.VMEM((nc, 8, width), F32),
+            pltpu.VMEM((nc, 2, width), F32),
             pltpu.VMEM((nc, hd, width), BF16),
             pltpu.VMEM((nc, hd, width), BF16),
             pltpu.VMEM((nc, hd, width), BF16),
-            pltpu.VMEM((nc, 8, width), F32),
-            pltpu.VMEM((nc, 8, width), F32),
+            pltpu.VMEM((nc, 2, width), F32),
+            pltpu.VMEM((nc, 2, width), F32),
             pltpu.VMEM((nc, CS, per, group, hd), BF16),
             dma((2,)),
             dma((2,)),

time: 38.2 us -> 34.5 us (0.903)
  Pallas kernels: 36.1 us -> 32.5 us
    pallas_call x1, Pallas kernels: 36.1 us -> 32.5 us  [on_device(): pl.pallas_call(functools.partial(kernel, n_ctx, owners, suf_dev, score_mu...]
where the time goes in v3:
time: 34.5 us; the launch traced here: 34.3 us
  Pallas kernels  32.5 us (94%)
  local copies, waits for them, and re-layouts  1.87 us (5%)
    pallas_call x1, Pallas kernels, on_device(): pl.pallas_call(functools.partial(kernel, n_ctx, owners, suf_dev, score_mu...  32.5 us
    unnamed x1, local copies, waits for them, and re-layouts  1.87 us

profile of v3, /device:TPU:0, one launch (start us, length us, event | category | flops | bytes accessed | tf_op | source)
XLA Modules:
  0.0 34.3 jit_solution(4351513421367040353)
XLA Ops:
  0.0 32.5 %shard_map.64 = bf16[4,16,4,8,128]{4,3,2,1,0:T(8,128)(2,1)} custom-call(bf16[4,16,4,8,128]{4,3,2,1,0:T(8,128)(2,1)} %q_ref.1, bf16[2,8192,128]{2,1,0:T(8,128)(2,1)} %bitcast.4, bf16[2,256,128]{2,1,0:T(8,128)(2,1)} %bitcast.5, bf16[4,2,64,128]{3,2,1,0:T(8,128)(2,1)} %bitcast.6, s32[4,32]{1,0:T(4,128)} %anc_ref.1, s32[1,32]{1,0:T(1,128)} %bitcast.7), custom_call_target="tpu_custom_call" | custom-call | tf_op jit(solution)/shard_map/pallas_call | solution.py:408
  32.5 1.9 %copy.8 = bf16[4,16,4,8,128]{4,3,2,1,0:T(8,128)(2,1)} copy(bf16[4,16,4,8,128]{4,3,2,1,0:T(8,128)(2,1)} %shard_map.64) | data formatting | bytes 1048576
